TPU v7x, 32 devices: a whole 2x2x4 slice. The times are simulated.
32 devices in a mesh: col: 2 (over x), row: 16 (over z, y, core).
Axes of the slice: x: 2, y: 2, z: 4, core: 2. Of those that a mesh axis runs over, the one named last changes fastest.
Arguments:
- residual: bfloat16 [1024, 2880], P('row'), may hold values from -6 to 6
- query_states: bfloat16 [1024, 4096], P('row', 'col'), may hold values from -48 to 48
- key_states: bfloat16 [1024, 512], P('row'), may hold values from -24 to 24
- value_states: bfloat16 [1024, 512], P('row'), may hold values from -6 to 6
- segment_ids: int32 [1024], P('row'), may hold values from 0 to 3, never falling along the last dimension, each value on 1 to 512 neighbouring positions
- sink_logits: float32 [64], P('col'), may hold values from -2 to 4
- w_out: bfloat16 [4096, 2880], P('col'), may hold values from -0.375 to 0.375
- norm_gain: float32 [2880], replicated, may hold values from 0.5 to 1.5
- expert_ids: int32 [1024, 4], P('row'), may hold values from 0 to 15, all different within a row; in each aligned block of 64 rows (0 to 63, 64 to 127, ...) at most 32 rows name the same one
- route_weight: float32 [1024, 4], P('row'), may hold values from 0.05 to 0.45
- w_gate_up: bfloat16 [16, 2, 2880, 2880], P('row', None, None, 'col'), may hold values from -0.109375 to 0.109375
- w_down: bfloat16 [16, 2880, 2880], P('row', 'col'), may hold values from -0.109375 to 0.109375
Outputs:
- layer_out: bfloat16 [1024, 2880], P('row', 'col')
Inputs may be any that keep to these rules, and one draw needn't show every extreme that they name: `expert_ids`: each token names 4 different experts; among the 64 tokens of one index of row no expert is named by more than 32 tokens, and in every draw some expert is named by exactly 32 of them. `segment_ids`: segment numbers never fall along the tokens.
All inputs are finite; a program needn't handle non-finite values.
Results may differ from a plain program's by a relative error of at most 0.018.
Values may be sent and summed in bfloat16 or wider, within the bound.
A program may use at most 128 MiB of HBM per device.

v0:
```python
import jax
import jax.numpy as jnp
from jax import lax
from jax.sharding import PartitionSpec as P

HEADS = 64
KV_HEADS = 8
HEAD_DIM = 64
WINDOW = 128
TOP = 4
epsilon = 1e-05
masked_score = -1e30


def shifted(shard, axis, by):
    size = lax.axis_size(axis)
    pairs = [(i, i + by) for i in range(size) if 0 <= i + by < size]
    return lax.ppermute(shard, axis, pairs)


def normalize(stream_rows, norm_gain):
    values32 = stream_rows.astype(jnp.float32)
    square_mean = jnp.mean(values32 * values32, axis=-1, keepdims=True)
    return (values32 * lax.rsqrt(square_mean + epsilon) * norm_gain).astype(jnp.bfloat16)


def attend(query_groups, key_groups, value_groups, allowed, sink_groups):
    scores = jnp.einsum(
        "tgjd,lgd->gjtl", query_groups, key_groups, preferred_element_type=jnp.float32
    )
    scores = scores * query_groups.shape[-1] ** (-0.5)
    scores = jnp.where(allowed[None, None], scores, masked_score)
    peak_score = jnp.maximum(jnp.max(scores, axis=-1, keepdims=True), sink_groups)
    numerator = jnp.exp(scores - peak_score)
    denominator = jnp.exp(sink_groups - peak_score) + jnp.sum(numerator, axis=-1, keepdims=True)
    weights = (numerator / denominator).astype(jnp.bfloat16)
    return jnp.einsum(
        "gjtl,lgd->tgjd", weights, value_groups, preferred_element_type=jnp.float32
    ).astype(jnp.bfloat16)


def local(
    residual,
    query_states,
    key_states,
    value_states,
    segment_ids,
    sink_logits,
    w_out,
    norm_gain,
    expert_ids,
    route_weight,
    w_gate_up,
    w_down,
):
    tok_rows = query_states.shape[0]
    row_count = lax.axis_size("row")
    col_count = lax.axis_size("col")
    row_index = lax.axis_index("row")
    col_index = lax.axis_index("col")
    local_heads = sink_logits.shape[0]
    group_size = HEADS // KV_HEADS
    if local_heads >= group_size:
        kv_count = local_heads // group_size
        kv_first = col_index * kv_count
    else:
        kv_count = 1
        kv_first = col_index * local_heads // group_size
    kv_width = kv_count * HEAD_DIM
    own_keys = lax.dynamic_slice_in_dim(key_states, kv_first * HEAD_DIM, kv_width, 1)
    own_values = lax.dynamic_slice_in_dim(value_states, kv_first * HEAD_DIM, kv_width, 1)
    shift_count = (WINDOW + tok_rows - 2) // tok_rows
    key_parts = []
    value_parts = []
    segment_parts = []
    start_parts = []
    for offset in range(shift_count, 0, -1):
        arrived = shifted((own_keys, own_values, segment_ids), "row", offset)
        key_parts.append(arrived[0])
        value_parts.append(arrived[1])
        segment_parts.append(arrived[2])
        start_parts.append((row_index - offset) * tok_rows)
    key_parts.append(own_keys)
    value_parts.append(own_values)
    segment_parts.append(segment_ids)
    start_parts.append(row_index * tok_rows)
    key_groups = jnp.concatenate(key_parts, 0).reshape(-1, kv_count, HEAD_DIM)
    value_groups = jnp.concatenate(value_parts, 0).reshape(-1, kv_count, HEAD_DIM)
    key_segments = jnp.concatenate(segment_parts, 0)
    positions = jnp.arange(tok_rows, dtype=jnp.int32)
    key_position = jnp.concatenate([start + positions for start in start_parts], 0)
    query_position = row_index * tok_rows + positions
    allowed = (key_position[None, :] >= 0) & (key_position[None, :] <= query_position[:, None])
    allowed = allowed & (key_position[None, :] > query_position[:, None] - WINDOW)
    allowed = allowed & (key_segments[None, :] == segment_ids[:, None])
    query_groups = query_states.reshape(tok_rows, kv_count, local_heads // kv_count, HEAD_DIM)
    sink_groups = sink_logits.reshape(kv_count, local_heads // kv_count, 1, 1)
    attended = attend(query_groups, key_groups, value_groups, allowed, sink_groups).reshape(
        tok_rows, local_heads * HEAD_DIM
    )
    partial_value = jnp.dot(attended, w_out, preferred_element_type=jnp.float32)
    feature_count = residual.shape[1] // col_count
    experts_all = w_gate_up.shape[0] * row_count
    slot_cap = max(2, 2 * TOP * tok_rows // experts_all)
    flat_ids = expert_ids.reshape(-1)
    expert_hot = (flat_ids[:, None] == jnp.arange(experts_all, dtype=jnp.int32)[None, :]).astype(
        jnp.int32
    )
    earlier = jnp.cumsum(expert_hot, axis=0) - expert_hot
    slot_of = jnp.sum(earlier * expert_hot, axis=1)
    slot_hot = (slot_of[:, None] == jnp.arange(slot_cap, dtype=jnp.int32)[None, :]).astype(
        jnp.float32
    )
    selector = jnp.einsum(
        "tke,tks->est",
        expert_hot.astype(jnp.float32).reshape(tok_rows, TOP, experts_all),
        slot_hot.reshape(tok_rows, TOP, slot_cap),
    )
    selector = selector.astype(jnp.bfloat16).reshape(experts_all * slot_cap, tok_rows)
    target = (flat_ids * slot_cap + slot_of).reshape(tok_rows, TOP)
    expert_gate_up = w_gate_up[0]
    expert_down = w_down[0]
    summed = lax.psum(partial_value.astype(jnp.bfloat16), "col").astype(jnp.float32)
    stream = (residual.astype(jnp.float32) + summed).astype(jnp.bfloat16)
    stream_part = lax.dynamic_slice_in_dim(stream, col_index * feature_count, feature_count, 1)
    source_rows = normalize(stream, norm_gain)
    packed = jnp.dot(selector, source_rows, preferred_element_type=jnp.float32).astype(jnp.bfloat16)
    gate_up = jnp.einsum(
        "scd,tdf->tscf",
        lax.all_to_all(
            packed.reshape(experts_all, slot_cap, source_rows.shape[1]),
            "row",
            split_axis=0,
            concat_axis=0,
            tiled=True,
        ),
        expert_gate_up,
        preferred_element_type=jnp.float32,
    )
    active = ((gate_up[1] + 1.0) * gate_up[0] * jax.nn.sigmoid(1.702 * gate_up[0])).astype(
        jnp.bfloat16
    )
    expert_partial = jnp.einsum(
        "scf,fd->scd", active, expert_down, preferred_element_type=jnp.float32
    )
    expert_result = lax.psum_scatter(
        expert_partial.astype(jnp.bfloat16), "col", scatter_dimension=2, tiled=True
    )
    returned = lax.all_to_all(expert_result, "row", split_axis=0, concat_axis=0, tiled=True)
    returned_rows = returned.reshape(experts_all * slot_cap, feature_count).astype(jnp.float32)
    picked = jnp.take(returned_rows, target, axis=0)
    expert_mix = jnp.sum(route_weight[:, :, None] * picked, axis=1)
    return (stream_part.astype(jnp.float32) + expert_mix).astype(jnp.bfloat16)


def solution(mesh):
    in_specs = (
        P("row", None),
        P("row", "col"),
        P("row", None),
        P("row", None),
        P("row"),
        P("col"),
        P("col", None),
        P(),
        P("row", None),
        P("row", None),
        P("row", None, None, "col"),
        P("row", "col", None),
    )
    out_specs = P("row", "col")
    return jax.shard_map(local, mesh=mesh, in_specs=in_specs, out_specs=out_specs, check_vma=False)
```

profile of v0, /device:TPU:13, one launch (start us, length us, event | category | flops | bytes accessed | tf_op | source)
XLA Modules:
  0.0 312.7 jit_solution(653327269411745198)
XLA Ops:
  6.5 3.3 %collective-permute-start.2 = (s32[64]{0:T(128)}, s32[64]{0:T(128)S(1)}, u32[]{:S(2)}, u32[]{:S(2)}) collective-permute-start(s32[64]{0:T(128)} %param.16), channel_id=1, source_target_pairs={{0,2},{1,3},{2,4},{3,5},{4,6},{5,7},{6,8},{7,9},{8,10},{9,11},{10,... | collective-permute-start | bytes 776 | tf_op jit(solution)/shard_map/ppermute | solution.py:18
  9.8 4.0 %collective-permute-start.3 = (s32[64]{0:T(128)}, s32[64]{0:T(128)S(1)}, u32[]{:S(2)}, u32[]{:S(2)}) collective-permute-start(s32[64]{0:T(128)} %param.16), channel_id=1, source_target_pairs={{0,1},{1,2},{2,3},{3,4},{4,5},{5,6},{6,7},{7,8},{8,9},{9,10},{10,1... | collective-permute-start | bytes 776 | tf_op jit(solution)/shard_map/ppermute | solution.py:18
  13.8 3.1 %collective-permute-start.4 = (bf16[64,256]{1,0:T(8,128)(2,1)S(1)}, bf16[64,256]{1,0:T(8,128)(2,1)S(1)}, u32[]{:S(2)}, u32[]{:S(2)}) collective-permute-start(bf16[64,256]{1,0:T(8,128)(2,1)S(1)} %constant_dynamic-slice_fusion), channel_id=1, source_target_pairs={{0,2},{1,3},{2,4},{3,5},{4,6},{5,7},{6,8},{7,9},{8,10},{9,11},{10,... | collective-permute-start | bytes 98312 | tf_op jit(solution)/shard_map/ppermute | solution.py:18
  17.0 2.2 collective-permute-start.5
  20.0 3.1 %collective-permute-start = (bf16[64,256]{1,0:T(8,128)(2,1)S(1)}, bf16[64,256]{1,0:T(8,128)(2,1)S(1)}, u32[]{:S(2)}, u32[]{:S(2)}) collective-permute-start(bf16[64,256]{1,0:T(8,128)(2,1)S(1)} %constant_dynamic-slice_fusion.1), channel_id=1, source_target_pairs={{0,2},{1,3},{2,4},{3,5},{4,6},{5,7},{6,8},{7,9},{8,10},{9,11},{10,... | collective-permute-start | bytes 98312 | tf_op jit(solution)/shard_map/ppermute | solution.py:18
  24.1 1.5 reshape.222
  26.9 2.3 collective-permute-start.1
  33.5 8.9 %convolution_convert_fusion.1 = bf16[64,2880]{1,0:T(8,128)(2,1)} fusion(bf16[64,2048]{0,1:T(8,128)(2,1)S(1)} %bitcast.74, bf16[2048,2880]{0,1:T(8,128)(2,1)} %param.18), kind=kOutput, calls=%fused_computation.8 | convolution fusion | flops 755159040 | bytes 12427264 | tf_op jit(solution)/shard_map/dot_general | solution.py:101
  43.8 22.9 %all-reduce.2.cloned.1.call-done = bf16[64,2880]{1,0:T(8,128)(2,1)} async-done(((bf16[64,2880]{1,0:T(8,128)(2,1)}), bf16[64,2880]{1,0:T(8,128)(2,1)}) %all-reduce.2.cloned.1.call-update) | async-done | bytes 368656 | tf_op jit(solution)/shard_map/psum | solution.py:123
  69.8 3.0 copy.56
  72.8 73.4 %all_to_all.10 = bf16[16,32,2880]{2,1,0:T(8,128)(2,1)S(1)} all-to-all(bf16[16,32,2880]{2,1,0:T(8,128)(2,1)} %bitcast.72), channel_id=1, replica_groups=mesh['col'=2,'row'=16] {'row'}, dimensions={0} | all-to-all | bytes 5898240 | tf_op jit(solution)/shard_map/all_to_all | solution.py:130
  146.2 15.2 %fusion.7 = f32[2,16,32,1440]{3,2,0,1:T(8,128)} fusion(bf16[1,2,2880,1440]{2,3,1,0:T(8,128)(2,1)} %param.22, bf16[16,32,2880]{2,1,0:T(8,128)(2,1)S(1)} %all_to_all.10), kind=kOutput, calls=%fused_computation.7 | convolution fusion | flops 8493465600 | bytes 25436160 | tf_op jit(solution)/shard_map/scd,tdf->tscf/dot_general | solution.py:128
  161.4 9.8 %fusion.4 = bf16[16,32,2880]{2,1,0:T(8,128)(2,1)S(1)} fusion(bf16[1,1440,2880]{2,1,0:T(8,128)(2,1)} %param.23, f32[2,16,32,1440]{3,2,0,1:T(8,128)} %fusion.7), kind=kOutput, calls=%fused_computation.5 | convolution fusion | flops 4254105600 | bytes 17141760 | tf_op jit(solution)/shard_map/scf,fd->scd/dot_general | solution.py:143
  171.2 12.1 %copy.61 = bf16[16,32,2880]{1,0,2:T(8,128)(2,1)} copy(bf16[16,32,2880]{2,1,0:T(8,128)(2,1)S(1)} %fusion.4) | data formatting | bytes 5898240
  183.3 16.3 %reshape.243 = bf16[2880,512]{1,0:T(8,128)(2,1)} reshape(bf16[2880,16,32]{2,1,0:T(8,128)(2,1)} %bitcast.70) | data formatting | bytes 5898240
  199.7 40.0 %reduce-scatter.4.cloned.1.call-done = bf16[1440,512]{1,0:T(8,128)(2,1)} async-done(((bf16[2880,512]{1,0:T(8,128)(2,1)}), bf16[1440,512]{1,0:T(8,128)(2,1)}) %reduce-scatter.4.cloned.1.call-update) | async-done | bytes 1474576
  239.7 7.7 %reshape.244 = bf16[1440,16,32]{2,1,0:T(8,128)(2,1)} reshape(bf16[1440,512]{1,0:T(8,128)(2,1)} %reduce-scatter.4.cloned.1.call-done) | data formatting | bytes 2949120
  247.4 7.2 %copy.62 = bf16[16,32,1440]{2,1,0:T(8,128)(2,1)} copy(bf16[16,32,1440]{1,0,2:T(8,128)(2,1)} %bitcast.71) | data formatting | bytes 2949120
  254.6 6.7 %all-to-all-start.1 = ((bf16[16,32,1440]{2,1,0:T(8,128)(2,1)}), bf16[16,32,1440]{2,1,0:T(8,128)(2,1)}, u32[]{:S(2)}, u32[]{:S(2)}) async-start(bf16[16,32,1440]{2,1,0:T(8,128)(2,1)} %copy.62), calls=%async_computation.1 | async-start | bytes 3145728 | tf_op jit(solution)/shard_map/all_to_all | solution.py:149
  261.8 35.8 %all-to-all-done.1 = bf16[16,32,1440]{2,1,0:T(8,128)(2,1)} async-done(((bf16[16,32,1440]{2,1,0:T(8,128)(2,1)}), bf16[16,32,1440]{2,1,0:T(8,128)(2,1)}, u32[]{:S(2)}, u32[]{:S(2)}) %all-to-all-start.1) | async-done | bytes 1474592 | tf_op jit(solution)/shard_map/all_to_all | solution.py:149
  297.6 1.8 bitcast_convert_fusion
  299.4 2.3 gather_fusion
  301.7 1.8 reshape.229
  303.6 1.4 multiply_reduce_fusion
  (66 shorter events, 13.0 us)
Async XLA Ops:
  6.5 7.3 %copy-start = (bf16[64,512]{1,0:T(8,128)(2,1)S(1)}, bf16[64,512]{1,0:T(8,128)(2,1)}, u32[]{:S(2)}) copy-start(bf16[64,512]{1,0:T(8,128)(2,1)} %param.14) | copy-start | bytes 196612
  6.5 60.2 %all-reduce.2.cloned.1.call-start = ((), (), s32[]{:S(2)}) async-start(), calls=%async_computation.3 | async-start | bytes 753664 | tf_op jit(solution)/shard_map/psum | solution.py:123
  6.5 20.4 %collective-permute-start.2 = (s32[64]{0:T(128)}, s32[64]{0:T(128)S(1)}, u32[]{:S(2)}, u32[]{:S(2)}) collective-permute-start(s32[64]{0:T(128)} %param.16), channel_id=1, source_target_pairs={{0,2},{1,3},{2,4},{3,5},{4,6},{5,7},{6,8},{7,9},{8,10},{9,11},{10,... | collective-permute-start | bytes 776 | tf_op jit(solution)/shard_map/ppermute | solution.py:18
  9.8 19.4 %collective-permute-start.3 = (s32[64]{0:T(128)}, s32[64]{0:T(128)S(1)}, u32[]{:S(2)}, u32[]{:S(2)}) collective-permute-start(s32[64]{0:T(128)} %param.16), channel_id=1, source_target_pairs={{0,1},{1,2},{2,3},{3,4},{4,5},{5,6},{6,7},{7,8},{8,9},{9,10},{10,1... | collective-permute-start | bytes 776 | tf_op jit(solution)/shard_map/ppermute | solution.py:18
  13.8 16.9 %collective-permute-start.4 = (bf16[64,256]{1,0:T(8,128)(2,1)S(1)}, bf16[64,256]{1,0:T(8,128)(2,1)S(1)}, u32[]{:S(2)}, u32[]{:S(2)}) collective-permute-start(bf16[64,256]{1,0:T(8,128)(2,1)S(1)} %constant_dynamic-slice_fusion), channel_id=1, source_target_pairs={{0,2},{1,3},{2,4},{3,5},{4,6},{5,7},{6,8},{7,9},{8,10},{9,11},{10,... | collective-permute-start | bytes 98312 | tf_op jit(solution)/shard_map/ppermute | solution.py:18
  17.0 13.7 %collective-permute-start.5 = (bf16[64,256]{1,0:T(8,128)(2,1)S(1)}, bf16[64,256]{1,0:T(8,128)(2,1)S(1)}, u32[]{:S(2)}, u32[]{:S(2)}) collective-permute-start(bf16[64,256]{1,0:T(8,128)(2,1)S(1)} %constant_dynamic-slice_fusion), channel_id=1, source_target_pairs={{0,1},{1,2},{2,3},{3,4},{4,5},{5,6},{6,7},{7,8},{8,9},{9,10},{10,1... | collective-permute-start | bytes 98312 | tf_op jit(solution)/shard_map/ppermute | solution.py:18
  20.0 12.3 %collective-permute-start = (bf16[64,256]{1,0:T(8,128)(2,1)S(1)}, bf16[64,256]{1,0:T(8,128)(2,1)S(1)}, u32[]{:S(2)}, u32[]{:S(2)}) collective-permute-start(bf16[64,256]{1,0:T(8,128)(2,1)S(1)} %constant_dynamic-slice_fusion.1), channel_id=1, source_target_pairs={{0,2},{1,3},{2,4},{3,5},{4,6},{5,7},{6,8},{7,9},{8,10},{9,11},{10,... | collective-permute-start | bytes 98312 | tf_op jit(solution)/shard_map/ppermute | solution.py:18
  26.9 5.4 %collective-permute-start.1 = (bf16[64,256]{1,0:T(8,128)(2,1)S(1)}, bf16[64,256]{1,0:T(8,128)(2,1)S(1)}, u32[]{:S(2)}, u32[]{:S(2)}) collective-permute-start(bf16[64,256]{1,0:T(8,128)(2,1)S(1)} %constant_dynamic-slice_fusion.1), channel_id=1, source_target_pairs={{0,1},{1,2},{2,3},{3,4},{4,5},{5,6},{6,7},{7,8},{8,9},{9,10},{10,1... | collective-permute-start | bytes 98312 | tf_op jit(solution)/shard_map/ppermute | solution.py:18
  33.5 33.3 %copy-start.4 = (bf16[64,2880]{1,0:T(8,128)(2,1)S(1)}, bf16[64,2880]{1,0:T(8,128)(2,1)}, u32[]{:S(2)}) copy-start(bf16[64,2880]{1,0:T(8,128)(2,1)} %param.12) | copy-start | bytes 1105924
  42.4 26.4 %copy-start.5 = (f32[2880]{0:T(1024)S(1)}, f32[2880]{0:T(1024)}, u32[]{:S(2)}) copy-start(f32[2880]{0:T(1024)} %param.19) | copy-start | bytes 34564
  42.4 197.3 %reduce-scatter.4.cloned.1.call-start = ((), (), s32[]{:S(2)}) async-start(), calls=%async_computation.4 | async-start | bytes 4423680
  68.0 0.8 copy-start.2
  254.6 6.7 %copy-start.6 = (s32[64,4]{0,1:T(4,128)S(1)}, s32[64,4]{0,1:T(4,128)}, u32[]{:S(2)}) copy-start(s32[64,4]{0,1:T(4,128)} %param.20) | copy-start | bytes 3076
  254.6 7.1 %copy-start.7 = (f32[64,4]{0,1:T(4,128)S(1)}, f32[64,4]{0,1:T(4,128)}, u32[]{:S(2)}) copy-start(f32[64,4]{0,1:T(4,128)} %param.21) | copy-start | bytes 3076
  254.6 42.9 %all-to-all-start.1 = ((bf16[16,32,1440]{2,1,0:T(8,128)(2,1)}), bf16[16,32,1440]{2,1,0:T(8,128)(2,1)}, u32[]{:S(2)}, u32[]{:S(2)}) async-start(bf16[16,32,1440]{2,1,0:T(8,128)(2,1)} %copy.62), calls=%async_computation.1 | async-start | bytes 3145728 | tf_op jit(solution)/shard_map/all_to_all | solution.py:149
  299.4 6.5 %copy-start.1 = (bf16[64,512]{1,0:T(8,128)(2,1)S(1)}, bf16[64,512]{1,0:T(8,128)(2,1)}, u32[]{:S(2)}) copy-start(bf16[64,512]{1,0:T(8,128)(2,1)} %param.14) | copy-start | bytes 196612
  301.7 3.3 %copy-start.3 = (bf16[64,2880]{1,0:T(8,128)(2,1)S(1)}, bf16[64,2880]{1,0:T(8,128)(2,1)}, u32[]{:S(2)}) copy-start(bf16[64,2880]{1,0:T(8,128)(2,1)} %copy-done.2) | copy-start | bytes 1105924
Sparse Core Ops, SparseCore 0:
  42.5 24.1 all-reduce.1
  199.8 39.8 reduce-scatter.3
where the time goes:
time: 314 us; the launch traced here: 313 us
  waiting for transfers between devices  98.8 us (31%)
  blocking collectives  73.4 us (23%)
  local copies, waits for them, and re-layouts  56.5 us (18%)
  matrix products  37.1 us (12%)
  starting transfers between devices  24.7 us (8%)
  between operations  13.7 us (4%)
  other arithmetic  8.42 us (3%)
    all_to_all x1, blocking collectives, local(): lax.all_to_all(packed.reshape(experts_all, slot_cap, source_rows.shape[1]...  73.4 us
    unnamed x22, local copies, waits for them, and re-layouts  45 us
    unnamed x3, waiting for transfers between devices  40.1 us
    all_to_all x1, waiting for transfers between devices, local(): lax.all_to_all(expert_result, 'row', split_axis=0, concat_axis=0, tiled=T...  35.8 us
    psum x1, waiting for transfers between devices, local(): lax.psum(partial_value.astype(jnp.bfloat16), 'col').astype(jnp.float32)  22.9 us
    ppermute x6, starting transfers between devices, shifted(): return lax.ppermute(shard, axis, pairs)  18 us
    dot_general x1, matrix products, local(): jnp.einsum('scd,tdf->tscf', lax.all_to_all(packed.reshape(experts_all, sl...  15.2 us
    dot_general x1, matrix products, local(): jnp.einsum('scf,fd->scd', active, expert_down, preferred_element_type=jnp...  9.8 us
  transfers between devices with their start and end apart: 9, of which 3 were waited for; matrix products, arithmetic and copies ran while one was open for 3% of the time, Pallas kernels for 0%

commit v1 on v0

--- a/solution.py
+++ b/solution.py
@@ -120,7 +120,9 @@
     target = (flat_ids * slot_cap + slot_of).reshape(tok_rows, TOP)
     expert_gate_up = w_gate_up[0]
     expert_down = w_down[0]
-    summed = lax.psum(partial_value.astype(jnp.bfloat16), "col").astype(jnp.float32)
+    summed = jnp.sum(lax.all_gather(partial_value.astype(jnp.bfloat16), "col"), axis=0).astype(
+        jnp.float32
+    )
     stream = (residual.astype(jnp.float32) + summed).astype(jnp.bfloat16)
     stream_part = lax.dynamic_slice_in_dim(stream, col_index * feature_count, feature_count, 1)
     source_rows = normalize(stream, norm_gain)

time: 314 us -> 300 us (0.955)
  waiting for transfers between devices: 98.8 us -> 76.7 us
  blocking collectives: 73.4 us -> 82.9 us
    psum x1 -> x0, waiting for transfers between devices: 22.9 us -> none  [local(): lax.psum(partial_value.astype(jnp.bfloat16), 'col').astype(jnp.float32)]
    all_gather x0 -> x1, blocking collectives: none -> 10.6 us  [local(): lax.all_gather(partial_value.astype(jnp.bfloat16), 'col')]
    unnamed x3 -> x2, waiting for transfers between devices: 40.1 us -> 40.9 us
  transfers between devices with their start and end apart: 9 -> 8, of which waited for: 3 -> 2; matrix products, arithmetic and copies ran while one was open for 3% -> 3% of each run, Pallas kernels for 0% -> 0%
where the time goes in v1:
time: 300 us; the launch traced here: 299 us
  blocking collectives  82.9 us (28%)
  waiting for transfers between devices  76.7 us (26%)
  local copies, waits for them, and re-layouts  56.5 us (19%)
  matrix products  36.3 us (12%)
  starting transfers between devices  24.7 us (8%)
  between operations  13.8 us (5%)
  other arithmetic  7.7 us (3%)
    all_to_all x1, blocking collectives, local(): lax.all_to_all(packed.reshape(experts_all, slot_cap, source_rows.shape[1]...  72.2 us
    unnamed x22, local copies, waits for them, and re-layouts  45 us
    unnamed x2, waiting for transfers between devices  40.9 us
    all_to_all x1, waiting for transfers between devices, local(): lax.all_to_all(expert_result, 'row', split_axis=0, concat_axis=0, tiled=T...  35.8 us
    ppermute x6, starting transfers between devices, shifted(): return lax.ppermute(shard, axis, pairs)  18 us
    dot_general x1, matrix products, local(): jnp.einsum('scd,tdf->tscf', lax.all_to_all(packed.reshape(experts_all, sl...  15.2 us
    all_gather x1, blocking collectives, local(): lax.all_gather(partial_value.astype(jnp.bfloat16), 'col')  10.6 us
    dot_general x1, matrix products, local(): jnp.einsum('scf,fd->scd', active, expert_down, preferred_element_type=jnp...  9.84 us
  transfers between devices with their start and end apart: 8, of which 2 were waited for; matrix products, arithmetic and copies ran while one was open for 3% of the time, Pallas kernels for 0%

profile of v1, /device:TPU:13, one launch (start us, length us, event | category | flops | bytes accessed | tf_op | source)
XLA Modules:
  0.0 298.6 jit_solution(17171265338819492494)
XLA Ops:
  6.5 3.3 %collective-permute-start.2 = (s32[64]{0:T(128)}, s32[64]{0:T(128)S(1)}, u32[]{:S(2)}, u32[]{:S(2)}) collective-permute-start(s32[64]{0:T(128)} %param.16), channel_id=1, source_target_pairs={{0,2},{1,3},{2,4},{3,5},{4,6},{5,7},{6,8},{7,9},{8,10},{9,11},{10,... | collective-permute-start | bytes 776 | tf_op jit(solution)/shard_map/ppermute | solution.py:18
  9.8 4.0 %collective-permute-start.3 = (s32[64]{0:T(128)}, s32[64]{0:T(128)S(1)}, u32[]{:S(2)}, u32[]{:S(2)}) collective-permute-start(s32[64]{0:T(128)} %param.16), channel_id=1, source_target_pairs={{0,1},{1,2},{2,3},{3,4},{4,5},{5,6},{6,7},{7,8},{8,9},{9,10},{10,1... | collective-permute-start | bytes 776 | tf_op jit(solution)/shard_map/ppermute | solution.py:18
  13.8 3.1 %collective-permute-start.4 = (bf16[64,256]{1,0:T(8,128)(2,1)S(1)}, bf16[64,256]{1,0:T(8,128)(2,1)S(1)}, u32[]{:S(2)}, u32[]{:S(2)}) collective-permute-start(bf16[64,256]{1,0:T(8,128)(2,1)S(1)} %constant_dynamic-slice_fusion), channel_id=1, source_target_pairs={{0,2},{1,3},{2,4},{3,5},{4,6},{5,7},{6,8},{7,9},{8,10},{9,11},{10,... | collective-permute-start | bytes 98312 | tf_op jit(solution)/shard_map/ppermute | solution.py:18
  17.0 2.2 collective-permute-start.5
  20.0 3.1 %collective-permute-start = (bf16[64,256]{1,0:T(8,128)(2,1)S(1)}, bf16[64,256]{1,0:T(8,128)(2,1)S(1)}, u32[]{:S(2)}, u32[]{:S(2)}) collective-permute-start(bf16[64,256]{1,0:T(8,128)(2,1)S(1)} %constant_dynamic-slice_fusion.1), channel_id=1, source_target_pairs={{0,2},{1,3},{2,4},{3,5},{4,6},{5,7},{6,8},{7,9},{8,10},{9,11},{10,... | collective-permute-start | bytes 98312 | tf_op jit(solution)/shard_map/ppermute | solution.py:18
  25.8 1.5 reshape.222
  28.3 2.3 collective-permute-start.1
  34.9 8.1 %convolution_convert_fusion.1 = bf16[64,2880]{1,0:T(8,128)(2,1)S(1)} fusion(bf16[64,2048]{0,1:T(8,128)(2,1)S(1)} %bitcast.76, bf16[2048,2880]{0,1:T(8,128)(2,1)} %param.18), kind=kOutput, calls=%fused_computation.8 | convolution fusion | flops 755159040 | bytes 12427264 | tf_op jit(solution)/shard_map/dot_general | solution.py:101
  43.0 10.6 %all-gather = bf16[128,2880]{1,0:T(8,128)(2,1)S(1)} all-gather(bf16[64,2880]{1,0:T(8,128)(2,1)S(1)} %convolution_convert_fusion.1), channel_id=2, replica_groups=mesh['col'=2,'row'=16] {'col'}, dimensions={0}, use_global_device_ids=true | all-gather | bytes 1105920 | tf_op jit(solution)/shard_map/all_gather | solution.py:123
  55.9 3.0 copy.56
  58.9 72.2 %all_to_all.10 = bf16[16,32,2880]{2,1,0:T(8,128)(2,1)S(1)} all-to-all(bf16[16,32,2880]{2,1,0:T(8,128)(2,1)} %bitcast.73), channel_id=1, replica_groups=mesh['col'=2,'row'=16] {'row'}, dimensions={0} | all-to-all | bytes 5898240 | tf_op jit(solution)/shard_map/all_to_all | solution.py:132
  131.1 15.2 %fusion.7 = f32[2,16,32,1440]{3,2,0,1:T(8,128)} fusion(bf16[1,2,2880,1440]{2,3,1,0:T(8,128)(2,1)} %param.22, bf16[16,32,2880]{2,1,0:T(8,128)(2,1)S(1)} %all_to_all.10), kind=kOutput, calls=%fused_computation.7 | convolution fusion | flops 8493465600 | bytes 25436160 | tf_op jit(solution)/shard_map/scd,tdf->tscf/dot_general | solution.py:130
  146.4 9.8 %fusion.4 = bf16[16,32,2880]{2,1,0:T(8,128)(2,1)S(1)} fusion(bf16[1,1440,2880]{2,1,0:T(8,128)(2,1)} %param.23, f32[2,16,32,1440]{3,2,0,1:T(8,128)} %fusion.7), kind=kOutput, calls=%fused_computation.5 | convolution fusion | flops 4254105600 | bytes 17141760 | tf_op jit(solution)/shard_map/scf,fd->scd/dot_general | solution.py:145
  156.2 12.1 %copy.61 = bf16[16,32,2880]{1,0,2:T(8,128)(2,1)} copy(bf16[16,32,2880]{2,1,0:T(8,128)(2,1)S(1)} %fusion.4) | data formatting | bytes 5898240
  168.3 16.3 %reshape.244 = bf16[2880,512]{1,0:T(8,128)(2,1)} reshape(bf16[2880,16,32]{2,1,0:T(8,128)(2,1)} %bitcast.71) | data formatting | bytes 5898240
  184.7 40.9 %reduce-scatter.4.cloned.1.call-done = bf16[1440,512]{1,0:T(8,128)(2,1)} async-done(((bf16[2880,512]{1,0:T(8,128)(2,1)}), bf16[1440,512]{1,0:T(8,128)(2,1)}) %reduce-scatter.4.cloned.1.call-update) | async-done | bytes 1474576
  225.6 7.7 %reshape.245 = bf16[1440,16,32]{2,1,0:T(8,128)(2,1)} reshape(bf16[1440,512]{1,0:T(8,128)(2,1)} %reduce-scatter.4.cloned.1.call-done) | data formatting | bytes 2949120
  233.3 7.2 %copy.62 = bf16[16,32,1440]{2,1,0:T(8,128)(2,1)} copy(bf16[16,32,1440]{1,0,2:T(8,128)(2,1)} %bitcast.72) | data formatting | bytes 2949120
  240.5 6.6 %all-to-all-start.1 = ((bf16[16,32,1440]{2,1,0:T(8,128)(2,1)}), bf16[16,32,1440]{2,1,0:T(8,128)(2,1)}, u32[]{:S(2)}, u32[]{:S(2)}) async-start(bf16[16,32,1440]{2,1,0:T(8,128)(2,1)} %copy.62), calls=%async_computation.1 | async-start | bytes 3145728 | tf_op jit(solution)/shard_map/all_to_all | solution.py:151
  247.7 35.8 %all-to-all-done.1 = bf16[16,32,1440]{2,1,0:T(8,128)(2,1)} async-done(((bf16[16,32,1440]{2,1,0:T(8,128)(2,1)}), bf16[16,32,1440]{2,1,0:T(8,128)(2,1)}, u32[]{:S(2)}, u32[]{:S(2)}) %all-to-all-start.1) | async-done | bytes 1474592 | tf_op jit(solution)/shard_map/all_to_all | solution.py:151
  283.4 1.8 bitcast_convert_fusion
  285.3 2.3 gather_fusion
  287.6 1.8 reshape.229
  289.4 1.4 multiply_reduce_fusion
  (65 shorter events, 12.2 us)
Async XLA Ops:
  6.5 7.3 %copy-start = (bf16[64,512]{1,0:T(8,128)(2,1)S(1)}, bf16[64,512]{1,0:T(8,128)(2,1)}, u32[]{:S(2)}) copy-start(bf16[64,512]{1,0:T(8,128)(2,1)} %param.14) | copy-start | bytes 196612
  6.5 219.0 %reduce-scatter.4.cloned.1.call-start = ((), (), s32[]{:S(2)}) async-start(), calls=%async_computation.3 | async-start | bytes 4423680
  6.5 21.7 %collective-permute-start.2 = (s32[64]{0:T(128)}, s32[64]{0:T(128)S(1)}, u32[]{:S(2)}, u32[]{:S(2)}) collective-permute-start(s32[64]{0:T(128)} %param.16), channel_id=1, source_target_pairs={{0,2},{1,3},{2,4},{3,5},{4,6},{5,7},{6,8},{7,9},{8,10},{9,11},{10,... | collective-permute-start | bytes 776 | tf_op jit(solution)/shard_map/ppermute | solution.py:18
  9.8 20.8 %collective-permute-start.3 = (s32[64]{0:T(128)}, s32[64]{0:T(128)S(1)}, u32[]{:S(2)}, u32[]{:S(2)}) collective-permute-start(s32[64]{0:T(128)} %param.16), channel_id=1, source_target_pairs={{0,1},{1,2},{2,3},{3,4},{4,5},{5,6},{6,7},{7,8},{8,9},{9,10},{10,1... | collective-permute-start | bytes 776 | tf_op jit(solution)/shard_map/ppermute | solution.py:18
  13.8 18.3 %collective-permute-start.4 = (bf16[64,256]{1,0:T(8,128)(2,1)S(1)}, bf16[64,256]{1,0:T(8,128)(2,1)S(1)}, u32[]{:S(2)}, u32[]{:S(2)}) collective-permute-start(bf16[64,256]{1,0:T(8,128)(2,1)S(1)} %constant_dynamic-slice_fusion), channel_id=1, source_target_pairs={{0,2},{1,3},{2,4},{3,5},{4,6},{5,7},{6,8},{7,9},{8,10},{9,11},{10,... | collective-permute-start | bytes 98312 | tf_op jit(solution)/shard_map/ppermute | solution.py:18
  17.0 15.1 %collective-permute-start.5 = (bf16[64,256]{1,0:T(8,128)(2,1)S(1)}, bf16[64,256]{1,0:T(8,128)(2,1)S(1)}, u32[]{:S(2)}, u32[]{:S(2)}) collective-permute-start(bf16[64,256]{1,0:T(8,128)(2,1)S(1)} %constant_dynamic-slice_fusion), channel_id=1, source_target_pairs={{0,1},{1,2},{2,3},{3,4},{4,5},{5,6},{6,7},{7,8},{8,9},{9,10},{10,1... | collective-permute-start | bytes 98312 | tf_op jit(solution)/shard_map/ppermute | solution.py:18
  20.0 13.7 %collective-permute-start = (bf16[64,256]{1,0:T(8,128)(2,1)S(1)}, bf16[64,256]{1,0:T(8,128)(2,1)S(1)}, u32[]{:S(2)}, u32[]{:S(2)}) collective-permute-start(bf16[64,256]{1,0:T(8,128)(2,1)S(1)} %constant_dynamic-slice_fusion.1), channel_id=1, source_target_pairs={{0,2},{1,3},{2,4},{3,5},{4,6},{5,7},{6,8},{7,9},{8,10},{9,11},{10,... | collective-permute-start | bytes 98312 | tf_op jit(solution)/shard_map/ppermute | solution.py:18
  28.3 5.4 %collective-permute-start.1 = (bf16[64,256]{1,0:T(8,128)(2,1)S(1)}, bf16[64,256]{1,0:T(8,128)(2,1)S(1)}, u32[]{:S(2)}, u32[]{:S(2)}) collective-permute-start(bf16[64,256]{1,0:T(8,128)(2,1)S(1)} %constant_dynamic-slice_fusion.1), channel_id=1, source_target_pairs={{0,1},{1,2},{2,3},{3,4},{4,5},{5,6},{6,7},{7,8},{8,9},{9,10},{10,1... | collective-permute-start | bytes 98312 | tf_op jit(solution)/shard_map/ppermute | solution.py:18
  34.9 19.0 %copy-start.4 = (bf16[64,2880]{1,0:T(8,128)(2,1)S(1)}, bf16[64,2880]{1,0:T(8,128)(2,1)}, u32[]{:S(2)}) copy-start(bf16[64,2880]{1,0:T(8,128)(2,1)} %param.12) | copy-start | bytes 1105924
  42.9 11.9 %copy-start.5 = (f32[2880]{0:T(1024)S(1)}, f32[2880]{0:T(1024)}, u32[]{:S(2)}) copy-start(f32[2880]{0:T(1024)} %param.19) | copy-start | bytes 34564
  54.1 0.8 copy-start.2
  240.5 6.7 %copy-start.6 = (s32[64,4]{0,1:T(4,128)S(1)}, s32[64,4]{0,1:T(4,128)}, u32[]{:S(2)}) copy-start(s32[64,4]{0,1:T(4,128)} %param.20) | copy-start | bytes 3076
  240.5 7.1 %copy-start.7 = (f32[64,4]{0,1:T(4,128)S(1)}, f32[64,4]{0,1:T(4,128)}, u32[]{:S(2)}) copy-start(f32[64,4]{0,1:T(4,128)} %param.21) | copy-start | bytes 3076
  240.5 42.9 %all-to-all-start.1 = ((bf16[16,32,1440]{2,1,0:T(8,128)(2,1)}), bf16[16,32,1440]{2,1,0:T(8,128)(2,1)}, u32[]{:S(2)}, u32[]{:S(2)}) async-start(bf16[16,32,1440]{2,1,0:T(8,128)(2,1)} %copy.62), calls=%async_computation.1 | async-start | bytes 3145728 | tf_op jit(solution)/shard_map/all_to_all | solution.py:151
  285.3 6.5 %copy-start.1 = (bf16[64,512]{1,0:T(8,128)(2,1)S(1)}, bf16[64,512]{1,0:T(8,128)(2,1)}, u32[]{:S(2)}) copy-start(bf16[64,512]{1,0:T(8,128)(2,1)} %param.14) | copy-start | bytes 196612
  287.6 3.3 %copy-start.3 = (bf16[64,2880]{1,0:T(8,128)(2,1)S(1)}, bf16[64,2880]{1,0:T(8,128)(2,1)}, u32[]{:S(2)}) copy-start(bf16[64,2880]{1,0:T(8,128)(2,1)} %copy-done.2) | copy-start | bytes 1105924
Sparse Core Ops, SparseCore 0:
  184.8 40.7 reduce-scatter.3
